TPU v7x, 32 devices: a whole 2x2x4 slice. The times are simulated.
32 devices in a mesh: ctx: 8 (over z, x), head: 4 (over y, core).
Axes of the slice: x: 2, y: 2, z: 4, core: 2. Of those that a mesh axis runs over, the one named last changes fastest.
Arguments:
- queries: bfloat16 [384, 5120], P('ctx', 'head'), as said below
- draft_keys: bfloat16 [384, 1024], P('ctx', 'head'), may hold values from -2.5 to 2.5
- draft_values: bfloat16 [384, 1024], P('ctx', 'head'), may hold values from -6 to 6
- cache_keys: bfloat16 [512, 128, 8, 128], P('ctx', None, 'head'), as said below
- cache_values: bfloat16 [512, 128, 8, 128], P('ctx', None, 'head'), may hold values from -6 to 6
- w_out: bfloat16 [5120, 5120], P('head', 'ctx'), may hold values from -0.078125 to 0.078125
- lengths: int32 [24], replicated, may hold values from 1 to 16384, as said below
- block_req: int32 [512], replicated, may hold values from 0 to 23, as said below
- block_idx: int32 [512], replicated, may hold values from -1 to 127
- move_dst: int32 [512], replicated, may hold values from -1 to 7, as said below
- draft_offs: int32 [24, 16], replicated, may hold values from 0 to 15, as said below
Outputs:
- mixed: bfloat16 [384, 5120], P('head', 'ctx')
- new_keys: bfloat16 [576, 128, 8, 128], P('ctx', None, 'head')
- new_values: bfloat16 [576, 128, 8, 128], P('ctx', None, 'head')
Inputs may be any that keep to these rules, and one draw needn't show every extreme that they name: queries lie within -6 to 6. cache_keys lie within -6 to 6. Request r has exactly ceil(lengths[r] / 128) blocks, numbered from 0, each in exactly one slot. Empty slots hold block_req 0; on each index of ctx the live slots come before the empty ones. `move_dst`: only live blocks move, never to their own index; at most 2 blocks go from one index of ctx to one other and at most 8 arrive at one index, both reached. draft_offs[r, t] <= t.
All inputs are finite; a program needn't handle non-finite values.
Results may differ from a plain program's by a relative error of at most 0.0051.
Values may be sent and summed in bfloat16 or wider, within the bound.
A program may use at most 128 MiB of HBM per device.

v0:
```python
import math

import jax
import jax.numpy as jnp
from jax import lax
from jax.sharding import PartitionSpec as P

CAP = 2


def live_tokens(lengths, slot_req, slot_idx, width):
    onehot = (slot_req[:, None] == jnp.arange(lengths.shape[0], dtype=jnp.int32)[None, :]).astype(
        jnp.int32
    )
    own_len = jnp.sum(onehot * lengths[None, :], axis=1) - slot_idx * width
    counts = jnp.where(slot_idx >= 0, jnp.clip(own_len, 0, width), 0)
    return jnp.arange(width, dtype=jnp.int32)[None, :] < counts[:, None]


def relocate(cache_keys, cache_values, move_dst, block_req, block_idx):
    blocks, width, kv_local, head_dim = cache_keys.shape
    nctx = lax.axis_size("ctx")
    rank = lax.axis_index("ctx")
    local_dst = lax.dynamic_slice_in_dim(move_dst, rank * blocks, blocks)
    local_req = lax.dynamic_slice_in_dim(block_req, rank * blocks, blocks)
    local_idx = lax.dynamic_slice_in_dim(block_idx, rank * blocks, blocks)
    line = jnp.arange(blocks, dtype=jnp.int32)
    earlier = (local_dst[None, :] == local_dst[:, None]) & (line[None, :] < line[:, None])
    place = jnp.sum(earlier.astype(jnp.int32), axis=1)
    target = jnp.where(local_dst >= 0, local_dst * CAP + place, nctx * CAP)
    flat_shape = (nctx * CAP, width, kv_local * head_dim)
    send_k = (
        jnp.zeros(flat_shape, cache_keys.dtype)
        .at[target]
        .set(cache_keys.reshape(blocks, width, kv_local * head_dim), mode="drop")
    )
    send_v = (
        jnp.zeros(flat_shape, cache_values.dtype)
        .at[target]
        .set(cache_values.reshape(blocks, width, kv_local * head_dim), mode="drop")
    )
    recv_k, recv_v = (
        lax.all_to_all(send_k, "ctx", split_axis=0, concat_axis=0, tiled=True),
        lax.all_to_all(send_v, "ctx", split_axis=0, concat_axis=0, tiled=True),
    )
    every = jnp.arange(move_dst.shape[0], dtype=jnp.int32)
    to_me = (move_dst == rank).astype(jnp.int32)
    before = jnp.cumsum(to_me) - to_me
    within = before - jnp.take(before, every // blocks * blocks)
    picks = (to_me[None, :] == 1) & (before[None, :] == jnp.arange(nctx, dtype=jnp.int32)[:, None])
    present = jnp.any(picks, axis=1)
    chosen = jnp.sum(jnp.where(picks, every[None, :], 0), axis=1)
    source_row = chosen // blocks * CAP + jnp.take(within, chosen)
    arrived_k = jnp.where(present[:, None, None], jnp.take(recv_k, source_row, axis=0), 0).reshape(
        nctx, width, kv_local, head_dim
    )
    arrived_v = jnp.where(present[:, None, None], jnp.take(recv_v, source_row, axis=0), 0).reshape(
        nctx, width, kv_local, head_dim
    )
    staying = local_dst < 0
    new_keys = jnp.concatenate(
        [jnp.where(staying[:, None, None, None], cache_keys, 0), arrived_k], axis=0
    )
    new_values = jnp.concatenate(
        [jnp.where(staying[:, None, None, None], cache_values, 0), arrived_v], axis=0
    )
    moved_req = jnp.concatenate(
        [jnp.where(staying, local_req, 0), jnp.where(present, jnp.take(block_req, chosen), 0)]
    )
    moved_idx = jnp.concatenate(
        [jnp.where(staying, local_idx, -1), jnp.where(present, jnp.take(block_idx, chosen), -1)]
    )
    return (new_keys, new_values, local_req, local_idx, moved_req, moved_idx)


def shards(
    queries,
    draft_keys,
    draft_values,
    cache_keys,
    cache_values,
    w_out,
    lengths,
    block_req,
    block_idx,
    move_dst,
    draft_offs,
):
    q_all, dk_all, dv_all = (
        lax.all_gather(queries, "ctx", axis=0, tiled=True),
        lax.all_gather(draft_keys, "ctx", axis=0, tiled=True),
        lax.all_gather(draft_values, "ctx", axis=0, tiled=True),
    )
    kv_local = cache_keys.shape[2]
    head_dim = cache_keys.shape[3]
    width = cache_keys.shape[1]
    requests = lengths.shape[0]
    drafts = draft_offs.shape[1]
    group = q_all.shape[1] // (kv_local * head_dim)
    tokens = requests * drafts
    scale = 1.0 / math.sqrt(head_dim)
    q_req = q_all.reshape(requests, drafts, kv_local, group, head_dim)
    dk_req = dk_all.reshape(requests, drafts, kv_local, head_dim)
    dv_req = dv_all.reshape(requests, drafts, kv_local, head_dim)
    new_keys, new_values, local_req, local_idx, moved_req, moved_idx = relocate(
        cache_keys, cache_values, move_dst, block_req, block_idx
    )
    keys_used, values_used, slot_req, slot_idx = (cache_keys, cache_values, local_req, local_idx)
    live = live_tokens(lengths, slot_req, slot_idx, width)
    q_slot = jnp.take(q_req, slot_req, axis=0)
    scores = (
        jnp.einsum("btkgd,bjkd->btkgj", q_slot, keys_used, preferred_element_type=jnp.float32)
        * scale
    )
    scores = jnp.where(live[:, None, None, None, :], scores, -jnp.inf)
    onehot = slot_req[None, :] == jnp.arange(requests, dtype=jnp.int32)[:, None]
    block_top = jnp.max(scores, axis=4)
    local_top = jnp.max(
        jnp.where(onehot[:, :, None, None, None], block_top[None], -jnp.inf), axis=1
    )
    cache_top = lax.pmax(local_top, "ctx")
    tpos = jnp.arange(drafts, dtype=jnp.int32)
    seen = (tpos[None, None, :] >= draft_offs[:, :, None]) & (
        tpos[None, None, :] <= tpos[None, :, None]
    )
    dscores = (
        jnp.einsum("rtkgd,rukd->rtkgu", q_req, dk_req, preferred_element_type=jnp.float32) * scale
    )
    dscores = jnp.where(seen[:, :, None, None, :], dscores, -jnp.inf)
    top = jnp.maximum(cache_top, jnp.max(dscores, axis=4))
    probs = jnp.where(
        live[:, None, None, None, :],
        jnp.exp(scores - jnp.take(top, slot_req, axis=0)[..., None]),
        0.0,
    )
    slot_denom = jnp.sum(probs, axis=4)
    slot_numer = jnp.einsum(
        "btkgj,bjkd->btkgd",
        probs.astype(jnp.bfloat16),
        values_used,
        preferred_element_type=jnp.float32,
    )
    onehot_f = onehot.astype(jnp.float32)
    cache_numer = jnp.einsum(
        "rb,btkgd->rtkgd", onehot_f, slot_numer, precision=lax.Precision.HIGHEST
    ).reshape(tokens, kv_local * group * head_dim)
    cache_denom = jnp.einsum(
        "rb,btkg->rtkg", onehot_f, slot_denom, precision=lax.Precision.HIGHEST
    ).reshape(tokens, kv_local * group)
    dprobs = jnp.where(seen[:, :, None, None, :], jnp.exp(dscores - top[..., None]), 0.0)
    draft_denom = jnp.sum(dprobs, axis=4).reshape(tokens, kv_local * group)
    draft_numer = jnp.einsum(
        "rtkgu,rukd->rtkgd", dprobs.astype(jnp.bfloat16), dv_req, preferred_element_type=jnp.float32
    ).reshape(tokens, kv_local * group * head_dim)
    total_numer, total_denom = lax.psum((cache_numer, cache_denom), "ctx")
    total_numer = total_numer + draft_numer
    total_denom = total_denom + draft_denom
    attn_all = (
        (total_numer.reshape(tokens, kv_local * group, head_dim) / total_denom[..., None])
        .reshape(tokens, -1)
        .astype(jnp.bfloat16)
    )
    mixed = lax.psum_scatter(
        jnp.dot(attn_all, w_out, preferred_element_type=jnp.float32),
        "head",
        scatter_dimension=0,
        tiled=True,
    ).astype(jnp.bfloat16)
    return (mixed, new_keys, new_values)


def solution(mesh):
    in_specs = (
        P("ctx", "head"),
        P("ctx", "head"),
        P("ctx", "head"),
        P("ctx", None, "head", None),
        P("ctx", None, "head", None),
        P("head", "ctx"),
        P(),
        P(),
        P(),
        P(),
        P(),
    )
    out_specs = (P("head", "ctx"), P("ctx", None, "head", None), P("ctx", None, "head", None))
    return jax.shard_map(shards, mesh=mesh, in_specs=in_specs, out_specs=out_specs, check_vma=False)
```

profile of v0, /device:TPU:0, one launch (start us, length us, event | category | flops | bytes accessed | tf_op | source)
XLA Modules:
  0.0 366.0 jit_solution(12599238339521299255)
XLA Ops:
  10.9 32.7 %all_gather.10 = bf16[384,256]{1,0:T(8,128)(2,1)S(1)} all-gather(bf16[48,256]{1,0:T(8,128)(2,1)} %param.14), channel_id=1, replica_groups=mesh['ctx'=8,'head'=4] {'ctx'}, dimensions={0}, use_global_device_ids=true | all-gather | bytes 221184 | tf_op jit(solution)/shard_map/all_gather | solution.py:91
  43.6 34.8 %all_gather.9 = bf16[384,1280]{1,0:T(8,128)(2,1)} all-gather(bf16[48,1280]{1,0:T(8,128)(2,1)} %param.13), channel_id=1, replica_groups=mesh['ctx'=8,'head'=4] {'ctx'}, dimensions={0}, use_global_device_ids=true | all-gather | bytes 1105920 | tf_op jit(solution)/shard_map/all_gather | solution.py:90
  81.0 3.3 fusion.24
  84.3 3.1 copy.83
  90.0 3.2 gather_fusion
  96.6 5.3 %bitcast_reduce_fusion = (f32[64,16,2,5]{1,3,2,0:T(8,128)S(1)}, f32[64,2,16,5,128]{4,2,3,1,0:T(8,128)}) fusion(pred[64,128]{1,0:T(8,128)(4,1)S(1)} %iota_compare_fusion.2, bf16[64,128,2,128,1]{3,2,1,0,4:T(2,128)(2,1)S(1)} %bitcast.65, bf16[64,16,2,5,128]{4,3,2,1,0:T(8,128)(2,1)S(1)} %broadcast_select_fusion.2), kind=kOutput, calls=%fused_computation.11 | convolution fusion | flops 339466240 | bytes 12107776 | tf_op jit(solution)/shard_map/btkgd,bjkd->btkgj/dot_general | solution.py:112
  102.7 40.0 %pmax.7 = f32[24,16,2,5]{1,3,2,0:T(8,128)S(1)} all-reduce(f32[24,16,2,5]{1,3,2,0:T(8,128)S(1)} %select_reduce_fusion), channel_id=1, replica_groups=mesh['ctx'=8,'head'=4] {'ctx'}, use_global_device_ids=true, to_apply=%region_3.4 | all-reduce | flops 3840 | bytes 30720 | tf_op jit(solution)/shard_map/pmax | solution.py:121
  143.6 4.8 %fusion.18 = f32[64,16,2,5,128]{4,1,3,2,0:T(8,128)S(1)} fusion(bf16[64,128,2,128,1]{3,2,1,0,4:T(2,128)(2,1)} %bitcast.64, f32[64,2,16,5,128]{4,2,3,1,0:T(8,128)} %get-tuple-element.19, f32[64,16,2,5]{1,3,2,0:T(8,128)S(1)} %broadcast_select_fusion.3, pred[64,128]{1,0:T(8,128)(4,1)S(1)} %iota_compare_fusion.2), kind=kOutput, calls=%fused_computation.33 | convolution fusion | flops 342097920 | bytes 14729216 | tf_op jit(solution)/shard_map/btkgj,bjkd->btkgd/dot_general | solution.py:137
  148.4 5.3 %fusion.2 = f32[24,16,2,5,128]{4,0,3,2,1:T(8,128)S(1)} fusion(f32[64,16,2,5,128]{4,1,3,2,0:T(8,128)S(1)} %fusion.18, s32[64]{0:T(128)S(1)} %get-tuple-element.11), kind=kOutput, calls=%fused_computation.14 | convolution fusion | flops 377488896 | bytes 7209216 | tf_op jit(solution)/shard_map/rb,btkgd->rtkgd/dot_general | solution.py:144
  155.9 3.8 %reshape.202 = f32[384,1280]{1,0:T(8,128)} reshape(f32[24,16,2,5,128]{4,3,2,1,0:T(8,128)} %copy.87) | data formatting | bytes 3932160 | tf_op jit(solution)/shard_map/reshape | solution.py:146
  159.7 7.7 %reshape.265 = bf16[64,128,256]{2,1,0:T(8,128)(2,1)} reshape(bf16[64,128,2,128]{3,2,1,0:T(2,128)(2,1)} %param.16) | data formatting | bytes 8388608 | tf_op jit(solution)/shard_map/reshape | solution.py:35
  169.5 11.1 %scatter_fusion = bf16[16,128,256]{2,1,0:T(8,128)(2,1)} fusion(bf16[16,128,256]{2,1,0:T(8,128)(2,1)} %broadcast.242.clone.1, s32[64]{0:T(128)S(1)} %compare_select_fusion.4, bf16[64,128,256]{2,1,0:T(8,128)(2,1)} %reshape.265), kind=kCustom, calls=%fused_computation.6 | custom fusion | bytes 12583168 | tf_op jit(solution)/shard_map/scatter | solution.py:35
  180.6 4.2 %all-to-all-start = ((bf16[16,128,256]{2,1,0:T(8,128)(2,1)}), bf16[16,128,256]{2,1,0:T(8,128)(2,1)}, u32[]{:S(2)}, u32[]{:S(2)}) async-start(bf16[16,128,256]{2,1,0:T(8,128)(2,1)} %scatter_fusion), calls=%async_computation.1 | async-start | bytes 2097152 | tf_op jit(solution)/shard_map/all_to_all | solution.py:43
  186.2 5.2 %fusion.8 = f32[64,16,2,5]{1,3,2,0:T(8,128)S(1)} fusion(f32[64,2,16,5,128]{4,2,3,1,0:T(8,128)} %get-tuple-element.19, f32[64,16,2,5]{1,3,2,0:T(8,128)S(1)} %broadcast_select_fusion.3, pred[64,128]{1,0:T(8,128)(4,1)S(1)} %iota_compare_fusion.2), kind=kLoop, calls=%fused_computation.24 | loop fusion | flops 6543360 | bytes 5332992 | tf_op jit(solution)/shard_map/reduce_sum | solution.py:136
  191.4 7.7 %reshape.273 = bf16[64,128,256]{2,1,0:T(8,128)(2,1)} reshape(bf16[64,128,2,128]{3,2,1,0:T(2,128)(2,1)} %param.17) | data formatting | bytes 8388608 | tf_op jit(solution)/shard_map/reshape | solution.py:40
  199.5 33.6 %all_gather.11 = bf16[384,256]{1,0:T(8,128)(2,1)} all-gather(bf16[48,256]{1,0:T(8,128)(2,1)S(1)} %copy-done.5), channel_id=1, replica_groups=mesh['ctx'=8,'head'=4] {'ctx'}, dimensions={0}, use_global_device_ids=true | all-gather | bytes 221184 | tf_op jit(solution)/shard_map/all_gather | solution.py:92
  245.1 3.9 %reshape.204 = f32[384,1280]{1,0:T(8,128)} reshape(f32[24,16,2,5,128]{4,3,2,1,0:T(8,128)} %copy.91) | data formatting | bytes 3932160 | tf_op jit(solution)/shard_map/reshape | solution.py:154
  249.0 38.3 %psum.15 = f32[384,10]{0,1:T(8,128)S(1)} all-reduce(f32[384,10]{0,1:T(8,128)S(1)} %reshape.205), channel_id=1, replica_groups=mesh['ctx'=8,'head'=4] {'ctx'}, use_global_device_ids=true, to_apply=%region_7.8 | all-reduce | flops 3840 | bytes 30720 | tf_op jit(solution)/shard_map/psum | solution.py:155
  291.8 3.5 gather_fusion.2
  297.2 10.8 %scatter_fusion.1 = bf16[16,128,256]{2,1,0:T(8,128)(2,1)} fusion(bf16[16,128,256]{2,1,0:T(8,128)(2,1)} %broadcast.242.clone, s32[64]{0:T(128)S(1)} %copy-done.12, bf16[64,128,256]{2,1,0:T(8,128)(2,1)} %reshape.273), kind=kCustom, calls=%fused_computation.7 | custom fusion | bytes 12583168 | tf_op jit(solution)/shard_map/scatter | solution.py:40
  308.1 3.6 all-to-all-start.1
  311.8 9.8 %broadcast_select_fusion = (bf16[64,128,2,128]{3,2,1,0:T(2,128)(2,1)}, bf16[64,128,2,128]{3,2,1,0:T(2,128)(2,1)}) fusion(bf16[64,128,2,128]{3,2,1,0:T(2,128)(2,1)} %param.17, pred[64]{0:T(512)(128)(4,1)S(1)} %copy-done.10, bf16[64,128,2,128]{3,2,1,0:T(2,128)(2,1)} %param.16), kind=kLoop, calls=%fused_computation.8 | loop fusion | flops 4194304 | bytes 16777280 | tf_op jit(solution)/shard_map/jit(_where)/select_n | solution.py:65
  321.6 4.6 %fusion.26 = f32[384,640]{1,0:T(8,128)} fusion(bf16[1280,640]{1,0:T(8,128)(2,1)S(1)} %copy-done, f32[384,1280]{1,0:T(8,128)} %copy.96, f32[384,1280]{1,0:T(8,128)} %all-reduce.2.cloned.1.call-done, f32[384,1280]{1,0:T(8,128)} %reshape.204), kind=kOutput, calls=%fused_computation.42 | convolution fusion | flops 630620160 | bytes 8519680 | tf_op jit(solution)/shard_map/dot_general | solution.py:164
  331.9 25.6 %pad_maximum_fusion = (bf16[72,128,2,128]{3,2,1,0:T(2,128)(2,1)}, bf16[72,128,2,128]{3,2,1,0:T(2,128)(2,1)}) fusion(bf16[8,128,2,128]{3,2,1,0:T(2,128)(2,1)S(1)} %reshape.210, bf16[64,128,2,128]{3,2,1,0:T(2,128)(2,1)} %get-tuple-element.17, bf16[8,128,2,128]{3,2,1,0:T(2,128)(2,1)S(1)} %reshape.212, bf16[64,128,2,128]{3,2,1,0:T(2,128)(2,1)} %get-tuple-element.16), kind=kLoop, calls=%fused_computation.17 | loop fusion | flops 4718592 | bytes 18874368 | tf_op jit(solution)/shard_map/concatenate | solution.py:61
  (95 shorter events, 45.8 us)
Async XLA Ops:
  7.2 314.4 %copy-start = (bf16[1280,640]{1,0:T(8,128)(2,1)S(1)}, bf16[1280,640]{1,0:T(8,128)(2,1)}, u32[]{:S(2)}) copy-start(bf16[1280,640]{1,0:T(8,128)(2,1)} %param.18) | copy-start | bytes 4915204
  7.2 314.4 %all-reduce.2.cloned.1.call-start = ((), (), s32[]{:S(2)}) async-start(), calls=%async_computation.3 | async-start | bytes 3932160 | tf_op jit(solution)/shard_map/psum | solution.py:155
  78.4 9.0 %copy-start.6 = (s32[24,16]{0,1:T(8,128)S(1)}, s32[24,16]{0,1:T(8,128)}, u32[]{:S(2)}) copy-start(s32[24,16]{0,1:T(8,128)} %param.23) | copy-start | bytes 4612
  87.5 0.6 copy-start.3
  89.9 3.2 copy-start.7
  93.2 3.4 copy-start.1
  159.7 7.8 %copy-start.9 = (s32[512]{0:T(512)S(1)}, s32[512]{0:T(512)}, u32[]{:S(2)}) copy-start(s32[512]{0:T(512)} %param.22) | copy-start | bytes 6148
  168.3 12.3 %copy-start.11 = (s32[64]{0:T(128)}, s32[64]{0:T(128)S(1)}, u32[]{:S(2)}) copy-start(s32[64]{0:T(128)S(1)} %compare_select_fusion.4) | copy-start | bytes 772
  180.6 127.5 %all-to-all-start = ((bf16[16,128,256]{2,1,0:T(8,128)(2,1)}), bf16[16,128,256]{2,1,0:T(8,128)(2,1)}, u32[]{:S(2)}, u32[]{:S(2)}) async-start(bf16[16,128,256]{2,1,0:T(8,128)(2,1)} %scatter_fusion), calls=%async_computation.1 | async-start | bytes 2097152 | tf_op jit(solution)/shard_map/all_to_all | solution.py:43
  191.4 8.2 %copy-start.5 = (bf16[48,256]{1,0:T(8,128)(2,1)S(1)}, bf16[48,256]{1,0:T(8,128)(2,1)}, u32[]{:S(2)}) copy-start(bf16[48,256]{1,0:T(8,128)(2,1)} %param.15) | copy-start | bytes 73732
  191.4 43.4 %copy-start.2 = (f32[24,2,16,16,5]{0,2,4,1,3:T(8,128)S(1)}, f32[24,2,16,16,5]{0,2,4,1,3:T(8,128)}, u32[]{:S(2)}) copy-start(f32[24,2,16,16,5]{0,2,4,1,3:T(8,128)} %copy.83) | copy-start | bytes 737284
  191.4 43.4 %copy-start.4 = (pred[24,16,16]{0,2,1:T(8,128)(4,1)S(1)}, pred[24,16,16]{0,2,1:T(8,128)(4,1)}, u32[]{:S(2)}) copy-start(pred[24,16,16]{0,2,1:T(8,128)(4,1)} %copy-done.3) | copy-start | bytes 18436
  249.0 46.3 %copy-start.8 = (pred[512]{0:T(512)(128)(4,1)S(1)}, pred[512]{0:T(512)(128)(4,1)}, u32[]{:S(2)}) copy-start(pred[512]{0:T(512)(128)(4,1)} %get-tuple-element.8) | copy-start | bytes 1540
  288.6 8.5 %copy-start.12 = (s32[64]{0:T(128)S(1)}, s32[64]{0:T(128)}, u32[]{:S(2)}) copy-start(s32[64]{0:T(128)} %copy-done.11) | copy-start | bytes 772
  297.2 14.6 %copy-start.10 = (pred[64]{0:T(512)(128)(4,1)S(1)}, pred[64]{0:T(512)(128)(4,1)}, u32[]{:S(2)}) copy-start(pred[64]{0:T(512)(128)(4,1)} %get-tuple-element.4) | copy-start | bytes 196
  308.1 20.8 %all-to-all-start.1 = ((bf16[16,128,256]{2,1,0:T(8,128)(2,1)}), bf16[16,128,256]{2,1,0:T(8,128)(2,1)S(1)}, u32[]{:S(2)}, u32[]{:S(2)}) async-start(bf16[16,128,256]{2,1,0:T(8,128)(2,1)} %scatter_fusion.1), calls=%async_computation.2 | async-start | bytes 2097152 | tf_op jit(solution)/shard_map/all_to_all | solution.py:44
  311.7 45.9 %reduce-scatter.2.cloned.1.call-start = ((), (), s32[]{:S(2)}) async-start(), calls=%async_computation.4 | async-start | bytes 1228800 | tf_op jit(solution)/shard_map/reduce_scatter | solution.py:163
Sparse Core Ops, SparseCore 0:
  159.8 113.6 all-reduce.1
  326.4 25.3 reduce-scatter.1
where the time goes:
time: 367 us; the launch traced here: 366 us
  blocking collectives  179 us (49%)
  local copies, waits for them, and re-layouts  81.7 us (22%)
  other arithmetic  57.6 us (16%)
  matrix products  25.2 us (7%)
  between operations  14.4 us (4%)
  starting transfers between devices  7.88 us (2%)
    pmax x1, blocking collectives, shards(): cache_top = lax.pmax(local_top, 'ctx')  40 us
    psum x1, blocking collectives, shards(): total_numer, total_denom = lax.psum((cache_numer, cache_denom), 'ctx')  38.3 us
    all_gather x1, blocking collectives, shards(): lax.all_gather(queries, 'ctx', axis=0, tiled=True)  34.8 us
    all_gather x1, blocking collectives, shards(): lax.all_gather(draft_values, 'ctx', axis=0, tiled=True)  33.6 us
    all_gather x1, blocking collectives, shards(): lax.all_gather(draft_keys, 'ctx', axis=0, tiled=True)  32.7 us
    concatenate x1, other arithmetic, relocate(): jnp.concatenate([jnp.where(staying[:, None, None, None], cache_keys, 0),...  25.6 us
    scatter x1, local copies, waits for them, and re-layouts, relocate(): send_k = jnp.zeros(flat_shape, cache_keys.dtype).at[target].set(cache_key...  11.1 us
    scatter x1, local copies, waits for them, and re-layouts, relocate(): send_v = jnp.zeros(flat_shape, cache_values.dtype).at[target].set(cache_v...  10.8 us
  transfers between devices with their start and end apart: 4, of which 0 were waited for; matrix products, arithmetic and copies ran while one was open for 32% of the time, Pallas kernels for 0%

commit v1 on v0

v1 whole, which is shorter than its diff:
```python
import functools
import math

import jax
import jax.numpy as jnp
from jax import lax
from jax.experimental import pallas as pl
from jax.experimental.pallas import tpu as pltpu
from jax.sharding import PartitionSpec as P

CAP = 2
STEP = 8
TOGETHER = 4
NEG = -1e30
MESH = pl.DeviceIdType.MESH
VMEM = pl.BlockSpec(memory_space=pltpu.VMEM)
SMEM = pl.BlockSpec(memory_space=pltpu.SMEM)
ANY = pl.BlockSpec(memory_space=pl.ANY)


def greet(axes):
    barrier = pltpu.get_barrier_semaphore()
    total = 0
    for axis, size in axes:
        me = lax.axis_index(axis)
        for d in range(1, size):
            pl.semaphore_signal(
                barrier, inc=1, device_id={axis: lax.rem(me + d, size)}, device_id_type=MESH
            )
        total += size - 1
    pl.semaphore_wait(barrier, total)


def remote(src, dst, send, recv, axis, to):
    return pltpu.make_async_remote_copy(
        src_ref=src, dst_ref=dst, send_sem=send, recv_sem=recv, device_id={axis: to}, device_id_type=MESH
    )


def spread(n, parts, send_sem, recv_sem, pair_send, pair_recv):
    me = lax.axis_index("ctx")
    half = n // 2
    row, side = me // 2, lax.rem(me, 2)
    partner = row * 2 + 1 - side
    started = []
    for a, (src, dst) in enumerate(parts):
        for d in range(1, half):
            to = lax.rem(row + d, half) * 2 + side
            c = remote(src, dst.at[me], send_sem.at[a, d], recv_sem.at[a, d], "ctx", to)
            c.start()
            started.append(c)
        c = remote(src, dst.at[me], pair_send.at[a, 0], pair_recv.at[a, 0], "ctx", partner)
        c.start()
        started.append(c)
    for d in range(1, half):
        for a, (src, dst) in enumerate(parts):
            origin = lax.rem(row + half - d, half) * 2 + side
            remote(src, dst.at[origin], send_sem.at[a, d], recv_sem.at[a, d], "ctx", partner).wait_recv()
            c = remote(
                dst.at[origin], dst.at[origin], pair_send.at[a, d], pair_recv.at[a, d], "ctx", partner
            )
            c.start()
            started.append(c)
    for d in range(half):
        for a, (src, dst) in enumerate(parts):
            origin = lax.rem(row + half - d, half) * 2 + 1 - side
            remote(src, dst.at[origin], pair_send.at[a, d], pair_recv.at[a, d], "ctx", partner).wait_recv()
    for c in started:
        c.wait_send()


def spread_sems(n, count):
    half = n // 2
    return [pltpu.SemaphoreType.DMA((count, half))] * 4


def gather_kernel(n, count, *refs):
    srcs, dsts, sems = refs[:count], refs[count : 2 * count], refs[2 * count :]
    local = sems[4]
    greet([("ctx", n)])
    me = lax.axis_index("ctx")
    own = []
    for a in range(count):
        c = pltpu.make_async_copy(srcs[a], dsts[a].at[me], local.at[a])
        c.start()
        own.append(c)
    spread(n, list(zip(srcs, dsts)), *sems[:4])
    for c in own:
        c.wait()


def gather_all(n, arrays):
    count = len(arrays)
    return pl.pallas_call(
        functools.partial(gather_kernel, n, count),
        out_shape=[jax.ShapeDtypeStruct((n,) + x.shape, x.dtype) for x in arrays],
        in_specs=[VMEM] * count,
        out_specs=[VMEM] * count,
        scratch_shapes=spread_sems(n, count) + [pltpu.SemaphoreType.DMA((count,))],
        compiler_params=pltpu.CompilerParams(collective_id=0, has_side_effects=True),
        name="gather_queries",
    )(*arrays)


def pack_kernel(blocks, n, rank_ref, dst_ref, k_ref, v_ref, out_ref, seen, sem):
    base = rank_ref[0] * blocks
    for d in range(n):
        seen[d] = 0

    def start(s, _):
        d = dst_ref[base + s]

        @pl.when(d >= 0)
        def _():
            row = d * CAP + seen[d]
            seen[d] = seen[d] + 1
            pltpu.make_async_copy(k_ref.at[s], out_ref.at[row, 0], sem).start()
            pltpu.make_async_copy(v_ref.at[s], out_ref.at[row, 1], sem).start()

        return 0

    lax.fori_loop(0, blocks, start, 0)

    def finish(s, _):
        @pl.when(dst_ref[base + s] >= 0)
        def _():
            pltpu.make_async_copy(k_ref.at[0], out_ref.at[0, 0], sem).wait()
            pltpu.make_async_copy(v_ref.at[0], out_ref.at[0, 1], sem).wait()

        return 0

    lax.fori_loop(0, blocks, finish, 0)


def pack(n, rank, move_dst, keys, values):
    blocks, rows, lanes = keys.shape
    return pl.pallas_call(
        functools.partial(pack_kernel, blocks, n),
        out_shape=jax.ShapeDtypeStruct((n * CAP, 2, rows, lanes), keys.dtype),
        in_specs=[SMEM, SMEM, ANY, ANY],
        out_specs=VMEM,
        scratch_shapes=[pltpu.SMEM((n,), jnp.int32), pltpu.SemaphoreType.DMA],
        name="pack_moves",
    )(rank, move_dst, keys, values)


def unpack_kernel(blocks, n, cnt_ref, recv_ref, nk_in, nv_in, nk_ref, nv_ref, stage, at, sem, out_sem):
    at[0] = 0
    for src in range(n):
        for j in range(CAP):

            @pl.when((j < cnt_ref[src]) & (at[0] < n))
            def _():
                for a in range(2):
                    pltpu.make_async_copy(
                        recv_ref.at[src * CAP + j, a], stage.at[a, at[0]], sem
                    ).start()
                at[0] = at[0] + 1

    total = at[0]

    def blank(k, _):
        stage[:, k] = jnp.zeros_like(stage[:, k])
        return 0

    lax.fori_loop(total, n, blank, 0)

    def finish(k, _):
        for a in range(2):
            pltpu.make_async_copy(recv_ref.at[0, a], stage.at[a, 0], sem).wait()
        return 0

    lax.fori_loop(0, total, finish, 0)
    outs = [
        pltpu.make_async_copy(stage.at[a], ref.at[pl.ds(blocks, n)], out_sem.at[a])
        for a, ref in enumerate((nk_ref, nv_ref))
    ]
    for c in outs:
        c.start()
    for c in outs:
        c.wait()


def unpack(n, blocks, arriving, received, new_keys, new_values):
    rows, lanes = new_keys.shape[1:]
    return pl.pallas_call(
        functools.partial(unpack_kernel, blocks, n),
        out_shape=[jax.ShapeDtypeStruct(x.shape, x.dtype) for x in (new_keys, new_values)],
        in_specs=[SMEM, ANY, ANY, ANY],
        out_specs=[ANY, ANY],
        input_output_aliases={2: 0, 3: 1},
        scratch_shapes=[
            pltpu.VMEM((2, n, rows, lanes), new_keys.dtype),
            pltpu.SMEM((1,), jnp.int32),
            pltpu.SemaphoreType.DMA,
            pltpu.SemaphoreType.DMA((2,)),
        ],
        name="place_moves",
    )(arriving, received, new_keys, new_values)


def attend_kernel(
    dims,
    rank_ref,
    req_ref,
    idx_ref,
    dst_ref,
    len_ref,
    dreq_ref,
    q_ref,
    k_ref,
    v_ref,
    dk_ref,
    dv_ref,
    bias_ref,
    nk_ref,
    nv_ref,
    o_ref,
    lse_ref,
    tok_ref,
    acc,
    top,
    den,
):
    blocks, width, kv, heads, hd, drafts, requests, own, aligned, steps = dims
    group = heads // kv
    qrows = heads * drafts
    i = pl.program_id(0)
    base = rank_ref[0] * blocks + i * STEP
    factor = math.log2(math.e) / math.sqrt(hd)
    nt = (((1,), (1,)), ((), ()))

    def query(r):
        q = q_ref[pl.ds(pl.multiple_of(r * drafts, drafts), drafts), :]
        return jnp.concatenate([q[:, h * hd : (h + 1) * hd] for h in range(heads)], axis=0)

    def part(s, v):
        m = jnp.max(s, axis=1, keepdims=True)
        p = jnp.exp2(s - m)
        total = jnp.sum(p, axis=1, keepdims=True)
        o = jnp.dot(p.astype(jnp.bfloat16), v, preferred_element_type=jnp.float32)
        return m, total, o

    def merge(r, m, total, o):
        old = top[r]
        new = jnp.maximum(old, m)
        a, b = jnp.exp2(old - new), jnp.exp2(m - new)
        top[r] = new
        den[r] = den[r] * a + total * b
        acc[r] = acc[r] * a + o * b

    @pl.when(i == 0)
    def _():
        row = lax.broadcasted_iota(jnp.int32, (qrows, kv * width), 0)
        col = lax.broadcasted_iota(jnp.int32, (qrows, kv * width), 1)
        tok_ref[...] = jnp.where(row // (group * drafts) == col % kv, col // kv, width)
        top[...] = jnp.full_like(top, NEG)
        den[...] = jnp.zeros_like(den)
        acc[...] = jnp.zeros_like(acc)
        for x in range(own):
            r = dreq_ref[x]
            place = x * drafts if aligned else pl.multiple_of(r * drafts, drafts)
            dk = dk_ref[pl.ds(place, drafts), :]
            dv = dv_ref[pl.ds(place, drafts), :]
            dk = jnp.concatenate([dk[:, g * hd : (g + 1) * hd] for g in range(kv)], axis=0)
            dv = jnp.concatenate([dv[:, g * hd : (g + 1) * hd] for g in range(kv)], axis=0)
            s = lax.dot_general(query(r), dk, nt, preferred_element_type=jnp.float32) * factor
            merge(r, *part(jnp.where(bias_ref[x] < 0, NEG, s), dv))

    for lo in range(0, STEP, TOGETHER):
        found = []
        for b in range(lo, lo + TOGETHER):
            r, x = req_ref[base + b], idx_ref[base + b]
            count = jnp.where(x >= 0, jnp.clip(len_ref[r] - x * width, 0, width), 0)
            s = lax.dot_general(query(r), k_ref[b], nt, preferred_element_type=jnp.float32) * factor
            s = jnp.where(tok_ref[...] < count, s, NEG)
            found.append((r,) + part(s, v_ref[b]))
        for r, m, total, o in found:
            merge(r, m, total, o)
    for b in range(STEP):
        away = dst_ref[base + b] >= 0

        @pl.when(away)
        def _():
            nk_ref[b] = jnp.zeros_like(nk_ref[b])
            nv_ref[b] = jnp.zeros_like(nv_ref[b])

        @pl.when(jnp.logical_not(away))
        def _():
            nk_ref[b] = k_ref[b]
            nv_ref[b] = v_ref[b]

    @pl.when(i == steps - 1)
    def _():
        lane = lax.broadcasted_iota(jnp.int32, (drafts, hd), 1)
        if o_ref.shape[0] > requests * drafts:
            rest = pl.ds(requests * drafts, o_ref.shape[0] - requests * drafts)
            o_ref[rest, :] = jnp.zeros_like(o_ref[rest, :])
            lse_ref[rest, :] = jnp.zeros_like(lse_ref[rest, :])

        def close(r, _):
            m, total = top[r], den[r]
            dead = total <= 0
            o = acc[r] * jnp.where(dead, 0.0, 1.0 / jnp.where(dead, 1.0, total))
            level = jnp.where(dead, NEG, m + jnp.log2(jnp.where(dead, 1.0, total)))
            rows = pl.ds(pl.multiple_of(r * drafts, drafts), drafts)
            packed = jnp.full((drafts, hd), NEG, jnp.float32)
            for h in range(heads):
                o_ref[rows, h * hd : (h + 1) * hd] = o[h * drafts : (h + 1) * drafts].astype(jnp.bfloat16)
                packed = jnp.where(lane == h, level[h * drafts : (h + 1) * drafts], packed)
            lse_ref[rows, :] = packed
            return 0

        lax.fori_loop(0, requests, close, 0)


def attend(n, rank, tables, dreq, q_all, keys, values, dk, dv, bias, kv, drafts, out_rows, aligned):
    blocks, rows, hd = keys.shape
    width = rows // kv
    block_req, block_idx, move_dst, lengths = tables
    requests = lengths.shape[0]
    heads = q_all.shape[1] // hd
    steps = blocks // STEP
    qrows = heads * drafts
    own = bias.shape[0]
    dims = (blocks, width, kv, heads, hd, drafts, requests, own, aligned, steps)
    whole = lambda x: pl.BlockSpec(x.shape, lambda i, *_: (0,) * x.ndim)
    slab = pl.BlockSpec((STEP, rows, hd), lambda i, *_: (i, 0, 0))
    grown = jax.ShapeDtypeStruct((blocks + n, rows, hd), keys.dtype)
    o = jax.ShapeDtypeStruct((out_rows, heads * hd), jnp.bfloat16)
    lse = jax.ShapeDtypeStruct((out_rows, hd), jnp.float32)
    return pl.pallas_call(
        functools.partial(attend_kernel, dims),
        out_shape=[grown, grown, o, lse],
        grid_spec=pltpu.PrefetchScalarGridSpec(
            num_scalar_prefetch=6,
            grid=(steps,),
            in_specs=[whole(q_all), slab, slab, whole(dk), whole(dv), whole(bias)],
            out_specs=[slab, slab, whole(o), whole(lse)],
            scratch_shapes=[
                pltpu.VMEM((qrows, rows), jnp.int32),
                pltpu.VMEM((requests, qrows, hd), jnp.float32),
                pltpu.VMEM((requests, qrows, hd), jnp.float32),
                pltpu.VMEM((requests, qrows, hd), jnp.float32),
            ],
        ),
        compiler_params=pltpu.CompilerParams(dimension_semantics=("arbitrary",)),
        cost_estimate=pl.CostEstimate(
            flops=4 * blocks * qrows * rows * hd, bytes_accessed=8 * blocks * rows * hd, transcendentals=0
        ),
        name="attend",
    )(rank, block_req, block_idx, move_dst, lengths, dreq, q_all, keys, values, dk, dv, bias)


def combine_kernel(dims, o_ref, lse_ref, w_ref, out_ref, got_o, got_l, attn_own, attn, part, got, *sems):
    n, nh, chunk, heads, hd, chunks, rows = dims
    os, orv, ls, lrv, hs, hr = sems[:6]
    local = sems[10]
    me = lax.axis_index("ctx")
    hme = lax.axis_index("head")
    greet([("ctx", n), ("head", nh)])
    sends = []
    for d in range(1, n):
        to = lax.rem(me + d, n)
        for src, dst, ss, rs in ((lse_ref, got_l, ls, lrv), (o_ref, got_o, os, orv)):
            c = remote(src.at[to], dst.at[d], ss.at[d], rs.at[d], "ctx", to)
            c.start()
            sends.append(c)
    for c in sends:
        c.wait_recv()
    levels = [lse_ref[me]] + [got_l[d] for d in range(1, n)]
    best = functools.reduce(jnp.maximum, levels)
    weights = [jnp.exp2(x - best) for x in levels]
    norm = 1.0 / functools.reduce(jnp.add, weights)
    weights = [x * norm for x in weights]
    for h in range(heads):
        cols = slice(h * hd, (h + 1) * hd)
        total = weights[0][:, h : h + 1] * o_ref[me, :, cols].astype(jnp.float32)
        for d in range(1, n):
            total += weights[d][:, h : h + 1] * got_o[d, :, cols].astype(jnp.float32)
        attn_own[:, cols] = total.astype(jnp.bfloat16)
    mine = pltpu.make_async_copy(attn_own, attn.at[me], local)
    mine.start()
    spread(n, [(attn_own, attn)], *sems[6:10])
    mine.wait()
    for c in sends:
        c.wait_send()
    w = w_ref[...]
    sends = []
    for d in range(1, nh):
        to = lax.rem(hme + d, nh)
        start = pl.multiple_of(to * rows, 16)
        part[d] = jnp.dot(
            attn_rows(attn, start, rows, chunk), w, preferred_element_type=jnp.float32
        ).astype(jnp.bfloat16)
        c = remote(part.at[d], got.at[d], hs.at[d], hr.at[d], "head", to)
        c.start()
        sends.append(c)
    total = jnp.dot(
        attn_rows(attn, pl.multiple_of(hme * rows, 16), rows, chunk), w, preferred_element_type=jnp.float32
    )
    for c in sends:
        c.wait_recv()
    for d in range(1, nh):
        total += got[d].astype(jnp.float32)
    out_ref[...] = total.astype(jnp.bfloat16)
    for c in sends:
        c.wait_send()


def attn_rows(attn, start, rows, chunk):
    piece = math.gcd(rows, chunk)
    out = []
    for x in range(rows // piece):
        at = start + x * piece
        out.append(attn[at // chunk, pl.ds(pl.multiple_of(lax.rem(at, chunk), 16), piece), :])
    return jnp.concatenate(out, axis=0)


def combine(n, nh, o, lse, w, tokens):
    _, chunk, cols = o.shape
    hd = lse.shape[2]
    heads = cols // hd
    rows = tokens // nh
    wide = w.shape[1]
    dims = (n, nh, chunk, heads, hd, tokens // chunk, rows)
    dma = pltpu.SemaphoreType.DMA
    return pl.pallas_call(
        functools.partial(combine_kernel, dims),
        out_shape=jax.ShapeDtypeStruct((rows, wide), jnp.bfloat16),
        in_specs=[VMEM] * 3,
        out_specs=VMEM,
        scratch_shapes=[
            pltpu.VMEM((n, chunk, cols), jnp.bfloat16),
            pltpu.VMEM((n, chunk, hd), jnp.float32),
            pltpu.VMEM((chunk, cols), jnp.bfloat16),
            pltpu.VMEM((n, chunk, cols), jnp.bfloat16),
            pltpu.VMEM((nh, rows, wide), jnp.bfloat16),
            pltpu.VMEM((nh, rows, wide), jnp.bfloat16),
            dma((n,)),
            dma((n,)),
            dma((n,)),
            dma((n,)),
            dma((nh,)),
            dma((nh,)),
        ]
        + spread_sems(n, 1)
        + [dma],
        compiler_params=pltpu.CompilerParams(collective_id=1, has_side_effects=True),
        name="combine",
    )(o, lse, w)


def shards(
    n,
    nh,
    queries,
    draft_keys,
    draft_values,
    cache_keys,
    cache_values,
    w_out,
    lengths,
    block_req,
    block_idx,
    move_dst,
    draft_offs,
):
    blocks, width, kv, hd = cache_keys.shape
    requests, drafts = draft_offs.shape
    tokens = requests * drafts
    local_tokens = queries.shape[0]
    heads = queries.shape[1] // hd
    me = lax.axis_index("ctx")
    rank = jnp.reshape(me, (1,)).astype(jnp.int32)
    keys = cache_keys.reshape(blocks, width * kv, hd)
    values = cache_values.reshape(blocks, width * kv, hd)
    sent = pack(n, rank, move_dst, keys, values)
    received = lax.all_to_all(sent, "ctx", split_axis=0, concat_axis=0, tiled=True)
    arriving = jnp.sum((move_dst.reshape(n, blocks) == me).astype(jnp.int32), axis=1)

    aligned = local_tokens % drafts == 0
    if aligned:
        own = local_tokens // drafts
        dreq = me * own + jnp.arange(own, dtype=jnp.int32)
        valid = jnp.full((own,), True)
        (q_all,) = gather_all(n, [queries])
        dk, dv = draft_keys, draft_values
    else:
        own = -(-requests // n)
        dreq = me + n * jnp.arange(own, dtype=jnp.int32)
        valid = dreq < requests
        dreq = jnp.where(valid, dreq, 0)
        q_all, dk, dv = gather_all(n, [queries, draft_keys, draft_values])
        dk, dv = dk.reshape(tokens, -1), dv.reshape(tokens, -1)
    q_all = q_all.reshape(tokens, heads * hd)
    offs = jnp.take(draft_offs, dreq, axis=0)
    line = jnp.arange(drafts, dtype=jnp.int32)
    seen = (line[None, None, :] >= offs[:, :, None]) & (line[None, None, :] <= line[None, :, None])
    seen = seen & valid[:, None, None]
    same = jnp.arange(heads)[:, None] // (heads // kv) == jnp.arange(kv)[None, :]
    bias = jnp.where(
        seen[:, None, :, None, :] & same[None, :, None, :, None], 0.0, -1.0
    ).astype(jnp.float32).reshape(own, heads * drafts, kv * drafts)
    chunk = -(-requests // n) * drafts
    new_keys, new_values, o, lse = attend(
        n,
        rank,
        (block_req, block_idx, move_dst, lengths),
        dreq,
        q_all,
        keys,
        values,
        dk,
        dv,
        bias,
        kv,
        drafts,
        n * chunk,
        aligned,
    )
    mixed = combine(n, nh, o.reshape(n, chunk, -1), lse.reshape(n, chunk, -1), w_out, tokens)
    new_keys, new_values = unpack(n, blocks, arriving, received, new_keys, new_values)
    shape = (blocks + n, width, kv, hd)
    return (mixed, new_keys.reshape(shape), new_values.reshape(shape))


def solution(mesh):
    in_specs = (
        P("ctx", "head"),
        P("ctx", "head"),
        P("ctx", "head"),
        P("ctx", None, "head", None),
        P("ctx", None, "head", None),
        P("head", "ctx"),
        P(),
        P(),
        P(),
        P(),
        P(),
    )
    out_specs = (P("head", "ctx"), P("ctx", None, "head", None), P("ctx", None, "head", None))
    body = functools.partial(shards, mesh.shape["ctx"], mesh.shape["head"])
    return jax.shard_map(body, mesh=mesh, in_specs=in_specs, out_specs=out_specs, check_vma=False)
```

time: 367 us -> 161 us (0.44)
  the two profiles are of different devices: /device:TPU:0 before, /device:TPU:1 now
where the time goes in v1:
time: 161 us; the launch traced here: 160 us
  Pallas kernels  147 us (91%)
  starting transfers between devices  6.36 us (4%)
  local copies, waits for them, and re-layouts  3.6 us (2%)
  other arithmetic  2.06 us (1%)
    pallas_call x1, Pallas kernels, combine(): pl.pallas_call(functools.partial(combine_kernel, dims), out_shape=jax.Sha...  64 us
    pallas_call x1, Pallas kernels, gather_all(): pl.pallas_call(functools.partial(gather_kernel, n, count), out_shape=[jax...  60.2 us
    pallas_call x1, Pallas kernels, attend(): pl.pallas_call(functools.partial(attend_kernel, dims), out_shape=[grown,...  16.3 us
    all_to_all x1, starting transfers between devices, shards(): lax.all_to_all(sent, 'ctx', split_axis=0, concat_axis=0, tiled=True)  6.36 us
    pallas_call x1, Pallas kernels, pack(): pl.pallas_call(functools.partial(pack_kernel, blocks, n), out_shape=jax.S...  3.59 us
  transfers between devices with their start and end apart: 1, of which 0 were waited for; matrix products, arithmetic and copies ran while one was open for 2% of the time, Pallas kernels for 88%

profile of v1, /device:TPU:1, one launch (start us, length us, event | category | flops | bytes accessed | tf_op | source)
XLA Modules:
  0.0 159.9 jit_solution(17243914817161311781)
XLA Ops:
  0.6 3.6 %pack_moves.1 = bf16[16,2,256,128]{3,2,1,0:T(8,128)(2,1)} custom-call(s32[1]{0:T(128)} %bitcast.rank_ref, s32[512]{0:T(512)} %dst_ref.3, bf16[64,256,128]{2,1,0:T(8,128)(2,1)} %bitcast.14, bf16[64,256,128]{2,1,0:T(8,128)(2,1)} %bitcast.16), custom_call_target="tpu_custom_call" | custom-call | tf_op jit(solution)/shard_map/pack_moves/pallas_call | solution.py:137
  4.2 0.0 copy-start.2
  4.2 0.0 copy-start.3
  4.3 6.4 %all-to-all-start = ((bf16[16,2,256,128]{3,2,1,0:T(8,128)(2,1)}), bf16[16,2,256,128]{3,2,1,0:T(8,128)(2,1)S(1)}, u32[]{:S(2)}, u32[]{:S(2)}) async-start(bf16[16,2,256,128]{3,2,1,0:T(8,128)(2,1)} %pack_moves.1), calls=%async_computation | async-start | bytes 4194304 | tf_op jit(solution)/shard_map/all_to_all | solution.py:479
  10.6 0.1 reshape.142
  10.7 0.1 copy.20
  10.8 0.1 and.55
  10.9 0.1 and.56
  11.0 0.1 copy.21
  11.2 0.6 gather_fusion
  11.8 0.1 broadcast_select_fusion
  11.9 0.1 and.52
  11.9 0.3 and.53
  12.2 0.2 copy.22
  12.4 60.2 %gather_queries.1 = bf16[8,48,1280]{2,1,0:T(8,128)(2,1)} custom-call(bf16[48,1280]{1,0:T(8,128)(2,1)} %refs_0_.1), custom_call_target="tpu_custom_call" | custom-call | tf_op jit(solution)/shard_map/gather_queries/pallas_call | solution.py:94
  72.6 0.6 iota_add_fusion.dreq_ref
  73.2 0.7 and_select_fusion.bias_ref
  73.9 16.3 %attend.1 = (bf16[72,256,128]{2,1,0:T(8,128)(2,1)}, bf16[72,256,128]{2,1,0:T(8,128)(2,1)}, bf16[384,1280]{1,0:T(8,128)(2,1)}, f32[384,128]{1,0:T(8,128)}) custom-call(s32[1]{0:T(128)} %bitcast.rank_ref, s32[512]{0:T(512)} %req_ref.1, s32[512]{0:T(512)} %idx_ref.1, s32[512]{0:T(512)} %dst_ref.3, s32[24]{0:T(128)} %len_ref.1, s32[3]{0:T(128)} %iota_add_fusion.dreq_ref, ...), custom_call_target="tpu_custom_call" | custom-call | flops 1342177280 | bytes 16777216 | tf_op jit(solution)/shard_map/attend/pallas_call | solution.py:332
  90.2 64.0 %combine.1 = bf16[96,640]{1,0:T(8,128)(2,1)} custom-call(bf16[8,48,1280]{2,1,0:T(8,128)(2,1)} %bitcast.21, f32[8,48,128]{2,1,0:T(8,128)} %bitcast.22, bf16[1280,640]{1,0:T(8,128)(2,1)} %w_ref.1), custom_call_target="tpu_custom_call" | custom-call | tf_op jit(solution)/shard_map/combine/pallas_call | solution.py:428
  154.2 0.6 reduce_sum.9.cnt_ref
  154.9 0.0 all-to-all-done.recv_ref
  154.9 1.3 copy-done
  156.2 3.0 %place_moves.1 = (bf16[72,256,128]{2,1,0:T(8,128)(2,1)}, bf16[72,256,128]{2,1,0:T(8,128)(2,1)}) custom-call(s32[8]{0:T(128)} %reduce_sum.9.cnt_ref, bf16[16,2,256,128]{3,2,1,0:T(8,128)(2,1)} %copy-done, bf16[72,256,128]{2,1,0:T(8,128)(2,1)} %get-tuple-element.11.nk_in, ...), custom_call_target="tpu_custom_call", output_to_operand_aliasing={{0}: (2, {}), {1}: (3, {})} | custom-call | tf_op jit(solution)/shard_map/place_moves/pallas_call | solution.py:186
  159.3 0.7 copy.26
  (13 shorter events, 0.1 us)
Async XLA Ops:
  4.2 6.4 %copy-start.2 = (s32[512]{0:T(512)S(1)}, s32[512]{0:T(512)}, u32[]{:S(2)}) copy-start(s32[512]{0:T(512)} %dst_ref.3) | copy-start | bytes 6148
  4.2 6.5 %copy-start.3 = (s32[24,16]{0,1:T(8,128)S(1)}, s32[24,16]{0,1:T(8,128)}, u32[]{:S(2)}) copy-start(s32[24,16]{0,1:T(8,128)} %param.21) | copy-start | bytes 4612
  4.3 150.6 %all-to-all-start = ((bf16[16,2,256,128]{3,2,1,0:T(8,128)(2,1)}), bf16[16,2,256,128]{3,2,1,0:T(8,128)(2,1)S(1)}, u32[]{:S(2)}, u32[]{:S(2)}) async-start(bf16[16,2,256,128]{3,2,1,0:T(8,128)(2,1)} %pack_moves.1), calls=%async_computation | async-start | bytes 4194304 | tf_op jit(solution)/shard_map/all_to_all | solution.py:479
  154.9 1.3 copy-start
  156.2 3.1 %copy-start.1 = (bf16[96,640]{1,0:T(8,128)(2,1)S(1)}, bf16[96,640]{1,0:T(8,128)(2,1)}, u32[]{:S(2)}) copy-start(bf16[96,640]{1,0:T(8,128)(2,1)} %combine.1) | copy-start | bytes 368644

commit v2 on v1

--- a/solution.py
+++ b/solution.py
@@ -352,57 +352,143 @@
     )(rank, block_req, block_idx, move_dst, lengths, dreq, q_all, keys, values, dk, dv, bias)
 
 
-def combine_kernel(dims, o_ref, lse_ref, w_ref, out_ref, got_o, got_l, attn_own, attn, part, got, *sems):
-    n, nh, chunk, heads, hd, chunks, rows = dims
-    os, orv, ls, lrv, hs, hr = sems[:6]
-    local = sems[10]
-    me = lax.axis_index("ctx")
-    hme = lax.axis_index("head")
-    greet([("ctx", n), ("head", nh)])
-    sends = []
-    for d in range(1, n):
-        to = lax.rem(me + d, n)
-        for src, dst, ss, rs in ((lse_ref, got_l, ls, lrv), (o_ref, got_o, os, orv)):
-            c = remote(src.at[to], dst.at[d], ss.at[d], rs.at[d], "ctx", to)
-            c.start()
-            sends.append(c)
-    for c in sends:
-        c.wait_recv()
-    levels = [lse_ref[me]] + [got_l[d] for d in range(1, n)]
+def merge_parts(parts, out, level_out, heads, hd):
+    levels = [level for _, level in parts]
     best = functools.reduce(jnp.maximum, levels)
     weights = [jnp.exp2(x - best) for x in levels]
-    norm = 1.0 / functools.reduce(jnp.add, weights)
+    mass = functools.reduce(jnp.add, weights)
+    norm = 1.0 / mass
     weights = [x * norm for x in weights]
     for h in range(heads):
         cols = slice(h * hd, (h + 1) * hd)
-        total = weights[0][:, h : h + 1] * o_ref[me, :, cols].astype(jnp.float32)
-        for d in range(1, n):
-            total += weights[d][:, h : h + 1] * got_o[d, :, cols].astype(jnp.float32)
-        attn_own[:, cols] = total.astype(jnp.bfloat16)
+        total = None
+        for (view, _), weight in zip(parts, weights):
+            term = weight[:, h : h + 1] * view[:, cols].astype(jnp.float32)
+            total = term if total is None else total + term
+        out[:, cols] = total.astype(jnp.bfloat16)
+    if level_out is not None:
+        level_out[...] = best + jnp.log2(mass)
+
+
+def combine_kernel(
+    dims, o_ref, lse_ref, w_ref, out_ref, near_o, near_l, pair_o, pair_l, far_o, far_l, attn_own, attn, part, got, mix, *sems
+):
+    n, nh, chunk, heads, hd, rows = dims
+    nos, nor, nls, nlr, fos, fo_r, fls, flr, hs, hr, ds, dr, ps, pr, local = sems
+    half = n // 2
+    me = lax.axis_index("ctx")
+    hme = lax.axis_index("head")
+    row, side = me // 2, lax.rem(me, 2)
+    partner = row * 2 + 1 - side
+    greet([("ctx", n), ("head", nh)])
+    order = list(range(1, half)) + [0]
+    sends = []
+
+    def near(d):
+        c = lax.rem(row + d, half) * 2 + 1 - side
+        return (
+            remote(lse_ref.at[c], near_l.at[d], nls.at[d], nlr.at[d], "ctx", partner),
+            remote(o_ref.at[c], near_o.at[d], nos.at[d], nor.at[d], "ctx", partner),
+        )
+
+    def far(d):
+        to = lax.rem(row + d, half) * 2 + side
+        return (
+            remote(pair_l.at[d], far_l.at[d], fls.at[d], flr.at[d], "ctx", to),
+            remote(pair_o.at[d], far_o.at[d], fos.at[d], fo_r.at[d], "ctx", to),
+        )
+
+    for d in order:
+        for c in near(d):
+            c.start()
+            sends.append(c)
+    for d in range(1, half):
+        for c in near(d):
+            c.wait_recv()
+        at = lax.rem(row + d, half) * 2 + side
+        merge_parts(
+            [(o_ref.at[at], lse_ref[at]), (near_o.at[d], near_l[d])], pair_o.at[d], pair_l.at[d], heads, hd
+        )
+        for c in far(d):
+            c.start()
+            sends.append(c)
+    for c in near(0):
+        c.wait_recv()
+    for d in range(1, half):
+        for c in far(d):
+            c.wait_recv()
+    merge_parts(
+        [(o_ref.at[me], lse_ref[me]), (near_o.at[0], near_l[0])]
+        + [(far_o.at[d], far_l[d]) for d in range(1, half)],
+        attn_own,
+        None,
+        heads,
+        hd,
+    )
     mine = pltpu.make_async_copy(attn_own, attn.at[me], local)
     mine.start()
-    spread(n, [(attn_own, attn)], *sems[6:10])
-    mine.wait()
-    for c in sends:
-        c.wait_send()
-    w = w_ref[...]
-    sends = []
-    for d in range(1, nh):
-        to = lax.rem(hme + d, nh)
-        start = pl.multiple_of(to * rows, 16)
-        part[d] = jnp.dot(
-            attn_rows(attn, start, rows, chunk), w, preferred_element_type=jnp.float32
-        ).astype(jnp.bfloat16)
-        c = remote(part.at[d], got.at[d], hs.at[d], hr.at[d], "head", to)
+
+    def direct(d):
+        to = lax.rem(row + d, half) * 2 + side
+        return remote(attn_own, attn.at[me], ds.at[d], dr.at[d], "ctx", to)
+
+    def landed(d, other):
+        origin = lax.rem(row + half - d, half) * 2 + (1 - side if other else side)
+        sem = (ps, pr) if other else (ds, dr)
+        remote(attn_own, attn.at[origin], sem[0].at[d], sem[1].at[d], "ctx", partner).wait_recv()
+
+    for d in range(1, half):
+        c = direct(d)
         c.start()
         sends.append(c)
-    total = jnp.dot(
-        attn_rows(attn, pl.multiple_of(hme * rows, 16), rows, chunk), w, preferred_element_type=jnp.float32
-    )
-    for c in sends:
+    c = remote(attn_own, attn.at[me], ps.at[0], pr.at[0], "ctx", partner)
+    c.start()
+    sends.append(c)
+
+    def pass_on(d):
+        landed(d, False)
+        origin = lax.rem(row + half - d, half) * 2 + side
+        c = remote(attn.at[origin], attn.at[origin], ps.at[d], pr.at[d], "ctx", partner)
+        c.start()
+        sends.append(c)
+
+    w = w_ref[...]
+
+    def project(j):
+        e = lax.rem(j + nh - hme, nh)
+        value = jnp.dot(
+            attn_rows(attn, pl.multiple_of(j * rows, 16), rows, chunk), w, preferred_element_type=jnp.float32
+        )
+
+        @pl.when(e == 0)
+        def _():
+            mix[...] = value
+
+        @pl.when(e != 0)
+        def _():
+            part[e] = value.astype(jnp.bfloat16)
+            remote(part.at[e], got.at[e], hs.at[e], hr.at[e], "head", j).start()
+
+    mine.wait()
+    if rows == 2 * chunk and nh == half:
+        for d in range(half):
+            if d + 1 < half:
+                pass_on(d + 1)
+            landed(d, True)
+            project(lax.rem(row + half - d, half))
+    else:
+        for d in range(1, half):
+            pass_on(d)
+        for d in range(half):
+            landed(d, True)
+        for d in range(nh):
+            project(lax.rem(hme + 1 + d, nh))
+    total = mix[...]
+    for e in range(1, nh):
+        c = remote(part.at[e], got.at[e], hs.at[e], hr.at[e], "head", lax.rem(hme + e, nh))
         c.wait_recv()
-    for d in range(1, nh):
-        total += got[d].astype(jnp.float32)
+        sends.append(c)
+        total += got[e].astype(jnp.float32)
     out_ref[...] = total.astype(jnp.bfloat16)
     for c in sends:
         c.wait_send()
@@ -423,28 +509,27 @@
     heads = cols // hd
     rows = tokens // nh
     wide = w.shape[1]
-    dims = (n, nh, chunk, heads, hd, tokens // chunk, rows)
+    half = n // 2
+    dims = (n, nh, chunk, heads, hd, rows)
     dma = pltpu.SemaphoreType.DMA
+    outs = pltpu.VMEM((half, chunk, cols), jnp.bfloat16)
+    levels = pltpu.VMEM((half, chunk, hd), jnp.float32)
     return pl.pallas_call(
         functools.partial(combine_kernel, dims),
         out_shape=jax.ShapeDtypeStruct((rows, wide), jnp.bfloat16),
         in_specs=[VMEM] * 3,
         out_specs=VMEM,
-        scratch_shapes=[
-            pltpu.VMEM((n, chunk, cols), jnp.bfloat16),
-            pltpu.VMEM((n, chunk, hd), jnp.float32),
+        scratch_shapes=[outs, levels] * 3
+        + [
             pltpu.VMEM((chunk, cols), jnp.bfloat16),
             pltpu.VMEM((n, chunk, cols), jnp.bfloat16),
             pltpu.VMEM((nh, rows, wide), jnp.bfloat16),
             pltpu.VMEM((nh, rows, wide), jnp.bfloat16),
-            dma((n,)),
-            dma((n,)),
-            dma((n,)),
-            dma((n,)),
-            dma((nh,)),
-            dma((nh,)),
+            pltpu.VMEM((rows, wide), jnp.float32),
         ]
-        + spread_sems(n, 1)
+        + [dma((half,))] * 8
+        + [dma((nh,))] * 2
+        + [dma((half,))] * 4
         + [dma],
         compiler_params=pltpu.CompilerParams(collective_id=1, has_side_effects=True),
         name="combine",
@@ -476,7 +561,6 @@
     keys = cache_keys.reshape(blocks, width * kv, hd)
     values = cache_values.reshape(blocks, width * kv, hd)
     sent = pack(n, rank, move_dst, keys, values)
-    received = lax.all_to_all(sent, "ctx", split_axis=0, concat_axis=0, tiled=True)
     arriving = jnp.sum((move_dst.reshape(n, blocks) == me).astype(jnp.int32), axis=1)
 
     aligned = local_tokens % drafts == 0
@@ -493,6 +577,8 @@
         dreq = jnp.where(valid, dreq, 0)
         q_all, dk, dv = gather_all(n, [queries, draft_keys, draft_values])
         dk, dv = dk.reshape(tokens, -1), dv.reshape(tokens, -1)
+    sent, q_all = lax.optimization_barrier((sent, q_all))
+    received = lax.all_to_all(sent, "ctx", split_axis=0, concat_axis=0, tiled=True)
     q_all = q_all.reshape(tokens, heads * hd)
     offs = jnp.take(draft_offs, dreq, axis=0)
     line = jnp.arange(drafts, dtype=jnp.int32)

time: 161 us -> 123 us (0.76)
  Pallas kernels: 147 us -> 111 us
  starting transfers between devices: 6.36 us -> 4.52 us
    pallas_call x1, Pallas kernels: 60.2 us -> 22.6 us  [gather_all(): pl.pallas_call(functools.partial(gather_kernel, n, count), out_shape=[jax...]
    pallas_call x1, Pallas kernels: 64 us -> 65.9 us  [combine(): pl.pallas_call(functools.partial(combine_kernel, dims), out_shape=jax.Sha...]
    all_to_all x1, starting transfers between devices: 6.36 us -> 4.52 us  [shards(): lax.all_to_all(sent, 'ctx', split_axis=0, concat_axis=0, tiled=True)]
  transfers between devices with their start and end apart: 1 -> 1, of which waited for: 0 -> 0; matrix products, arithmetic and copies ran while one was open for 2% -> 3% of each run, Pallas kernels for 88% -> 68%
where the time goes in v2:
time: 123 us; the launch traced here: 122 us
  Pallas kernels  111 us (90%)
  starting transfers between devices  4.52 us (4%)
  local copies, waits for them, and re-layouts  3.6 us (3%)
  other arithmetic  2.06 us (2%)
    pallas_call x1, Pallas kernels, combine(): pl.pallas_call(functools.partial(combine_kernel, dims), out_shape=jax.Sha...  65.9 us
    pallas_call x1, Pallas kernels, gather_all(): pl.pallas_call(functools.partial(gather_kernel, n, count), out_shape=[jax...  22.6 us
    pallas_call x1, Pallas kernels, attend(): pl.pallas_call(functools.partial(attend_kernel, dims), out_shape=[grown,...  16.4 us
    all_to_all x1, starting transfers between devices, shards(): lax.all_to_all(sent, 'ctx', split_axis=0, concat_axis=0, tiled=True)  4.52 us
    pallas_call x1, Pallas kernels, pack(): pl.pallas_call(functools.partial(pack_kernel, blocks, n), out_shape=jax.S...  4.01 us
  transfers between devices with their start and end apart: 1, of which 0 were waited for; matrix products, arithmetic and copies ran while one was open for 3% of the time, Pallas kernels for 68%

profile of v2, /device:TPU:1, one launch (start us, length us, event | category | flops | bytes accessed | tf_op | source)
XLA Modules:
  0.0 121.9 jit_solution(8982954412536156692)
XLA Ops:
  0.6 22.6 %gather_queries.1 = bf16[8,48,1280]{2,1,0:T(8,128)(2,1)} custom-call(bf16[48,1280]{1,0:T(8,128)(2,1)} %refs_0_.1), custom_call_target="tpu_custom_call" | custom-call | tf_op jit(solution)/shard_map/gather_queries/pallas_call | solution.py:94
  23.2 4.0 %pack_moves.1 = bf16[16,2,256,128]{3,2,1,0:T(8,128)(2,1)} custom-call(s32[1]{0:T(128)} %bitcast.rank_ref, s32[512]{0:T(512)} %dst_ref.3, bf16[64,256,128]{2,1,0:T(8,128)(2,1)} %bitcast.14, bf16[64,256,128]{2,1,0:T(8,128)(2,1)} %bitcast.16), custom_call_target="tpu_custom_call" | custom-call | tf_op jit(solution)/shard_map/pack_moves/pallas_call | solution.py:137
  27.2 0.0 copy-start.2
  27.3 0.0 copy-start.3
  27.3 4.5 %all-to-all-start = ((bf16[16,2,256,128]{3,2,1,0:T(8,128)(2,1)}), bf16[16,2,256,128]{3,2,1,0:T(8,128)(2,1)S(1)}, u32[]{:S(2)}, u32[]{:S(2)}) async-start(bf16[16,2,256,128]{3,2,1,0:T(8,128)(2,1)} %pack_moves.1), calls=%async_computation | async-start | bytes 4194304 | tf_op jit(solution)/shard_map/all_to_all | solution.py:581
  31.8 0.1 reshape.142
  31.9 0.1 copy.20
  32.0 0.1 and.55
  32.1 0.1 and.56
  32.2 0.1 copy.21
  32.4 0.6 gather_fusion
  33.0 0.1 broadcast_select_fusion
  33.0 0.1 and.52
  33.1 0.3 and.53
  33.4 0.2 copy.22
  33.6 0.6 iota_add_fusion.dreq_ref
  34.2 0.7 and_select_fusion.bias_ref
  34.9 16.4 %attend.1 = (bf16[72,256,128]{2,1,0:T(8,128)(2,1)}, bf16[72,256,128]{2,1,0:T(8,128)(2,1)}, bf16[384,1280]{1,0:T(8,128)(2,1)}, f32[384,128]{1,0:T(8,128)}) custom-call(s32[1]{0:T(128)} %bitcast.rank_ref, s32[512]{0:T(512)} %req_ref.1, s32[512]{0:T(512)} %idx_ref.1, s32[512]{0:T(512)} %dst_ref.3, s32[24]{0:T(128)} %len_ref.1, s32[3]{0:T(128)} %iota_add_fusion.dreq_ref, ...), custom_call_target="tpu_custom_call" | custom-call | flops 1342177280 | bytes 16777216 | tf_op jit(solution)/shard_map/attend/pallas_call | solution.py:332
  51.3 65.9 %combine.1 = bf16[96,640]{1,0:T(8,128)(2,1)} custom-call(bf16[8,48,1280]{2,1,0:T(8,128)(2,1)} %bitcast.21, f32[8,48,128]{2,1,0:T(8,128)} %bitcast.22, bf16[1280,640]{1,0:T(8,128)(2,1)} %w_ref.1), custom_call_target="tpu_custom_call" | custom-call | tf_op jit(solution)/shard_map/combine/pallas_call | solution.py:517
  117.2 0.6 reduce_sum.9.cnt_ref
  117.8 0.0 all-to-all-done.recv_ref
  117.8 1.3 %copy-done = bf16[16,2,256,128]{3,2,1,0:T(8,128)(2,1)} copy-done((bf16[16,2,256,128]{3,2,1,0:T(8,128)(2,1)}, bf16[16,2,256,128]{3,2,1,0:T(8,128)(2,1)S(1)}, u32[]{:S(2)}) %copy-start) | copy-done | bytes 2097176
  119.2 2.0 %place_moves.1 = (bf16[72,256,128]{2,1,0:T(8,128)(2,1)}, bf16[72,256,128]{2,1,0:T(8,128)(2,1)}) custom-call(s32[8]{0:T(128)} %reduce_sum.9.cnt_ref, bf16[16,2,256,128]{3,2,1,0:T(8,128)(2,1)} %copy-done, bf16[72,256,128]{2,1,0:T(8,128)(2,1)} %get-tuple-element.15.nk_in, ...), custom_call_target="tpu_custom_call", output_to_operand_aliasing={{0}: (2, {}), {1}: (3, {})} | custom-call | tf_op jit(solution)/shard_map/place_moves/pallas_call | solution.py:186
  121.2 0.7 copy.26
  (13 shorter events, 0.1 us)
Async XLA Ops:
  27.2 4.5 %copy-start.2 = (s32[512]{0:T(512)S(1)}, s32[512]{0:T(512)}, u32[]{:S(2)}) copy-start(s32[512]{0:T(512)} %dst_ref.3) | copy-start | bytes 6148
  27.3 4.6 %copy-start.3 = (s32[24,16]{0,1:T(8,128)S(1)}, s32[24,16]{0,1:T(8,128)}, u32[]{:S(2)}) copy-start(s32[24,16]{0,1:T(8,128)} %param.21) | copy-start | bytes 4612
  27.3 90.6 %all-to-all-start = ((bf16[16,2,256,128]{3,2,1,0:T(8,128)(2,1)}), bf16[16,2,256,128]{3,2,1,0:T(8,128)(2,1)S(1)}, u32[]{:S(2)}, u32[]{:S(2)}) async-start(bf16[16,2,256,128]{3,2,1,0:T(8,128)(2,1)} %pack_moves.1), calls=%async_computation | async-start | bytes 4194304 | tf_op jit(solution)/shard_map/all_to_all | solution.py:581
  117.8 1.3 %copy-start = (bf16[16,2,256,128]{3,2,1,0:T(8,128)(2,1)}, bf16[16,2,256,128]{3,2,1,0:T(8,128)(2,1)S(1)}, u32[]{:S(2)}) copy-start(bf16[16,2,256,128]{3,2,1,0:T(8,128)(2,1)S(1)} %all-to-all-done.recv_ref) | copy-start | bytes 6291460
  119.2 2.0 %copy-start.1 = (bf16[96,640]{1,0:T(8,128)(2,1)S(1)}, bf16[96,640]{1,0:T(8,128)(2,1)}, u32[]{:S(2)}) copy-start(bf16[96,640]{1,0:T(8,128)(2,1)} %combine.1) | copy-start | bytes 368644

commit v3 on v2

--- a/solution.py
+++ b/solution.py
@@ -46,25 +46,25 @@
     for a, (src, dst) in enumerate(parts):
         for d in range(1, half):
             to = lax.rem(row + d, half) * 2 + side
-            c = remote(src, dst.at[me], send_sem.at[a, d], recv_sem.at[a, d], "ctx", to)
+            c = remote(src, dst(me), send_sem.at[a, d], recv_sem.at[a, d], "ctx", to)
             c.start()
             started.append(c)
-        c = remote(src, dst.at[me], pair_send.at[a, 0], pair_recv.at[a, 0], "ctx", partner)
+        c = remote(src, dst(me), pair_send.at[a, 0], pair_recv.at[a, 0], "ctx", partner)
         c.start()
         started.append(c)
     for d in range(1, half):
         for a, (src, dst) in enumerate(parts):
             origin = lax.rem(row + half - d, half) * 2 + side
-            remote(src, dst.at[origin], send_sem.at[a, d], recv_sem.at[a, d], "ctx", partner).wait_recv()
+            remote(src, dst(origin), send_sem.at[a, d], recv_sem.at[a, d], "ctx", partner).wait_recv()
             c = remote(
-                dst.at[origin], dst.at[origin], pair_send.at[a, d], pair_recv.at[a, d], "ctx", partner
+                dst(origin), dst(origin), pair_send.at[a, d], pair_recv.at[a, d], "ctx", partner
             )
             c.start()
             started.append(c)
     for d in range(half):
         for a, (src, dst) in enumerate(parts):
             origin = lax.rem(row + half - d, half) * 2 + 1 - side
-            remote(src, dst.at[origin], pair_send.at[a, d], pair_recv.at[a, d], "ctx", partner).wait_recv()
+            remote(src, dst(origin), pair_send.at[a, d], pair_recv.at[a, d], "ctx", partner).wait_recv()
     for c in started:
         c.wait_send()
 
@@ -72,6 +72,12 @@
 def spread_sems(n, count):
     half = n // 2
     return [pltpu.SemaphoreType.DMA((count, half))] * 4
+
+
+def pieces(width):
+    if width % 256:
+        return [slice(0, width)]
+    return [slice(0, width // 2), slice(width // 2, width)]
 
 
 def gather_kernel(n, count, *refs):
@@ -84,7 +90,11 @@
         c = pltpu.make_async_copy(srcs[a], dsts[a].at[me], local.at[a])
         c.start()
         own.append(c)
-    spread(n, list(zip(srcs, dsts)), *sems[:4])
+    parts = []
+    for src, dst in zip(srcs, dsts):
+        for cols in pieces(src.shape[1]):
+            parts.append((src.at[:, cols], lambda o, dst=dst, cols=cols: dst.at[o, :, cols]))
+    spread(n, parts, *sems[:4])
     for c in own:
         c.wait()
 
@@ -96,7 +106,8 @@
         out_shape=[jax.ShapeDtypeStruct((n,) + x.shape, x.dtype) for x in arrays],
         in_specs=[VMEM] * count,
         out_specs=[VMEM] * count,
-        scratch_shapes=spread_sems(n, count) + [pltpu.SemaphoreType.DMA((count,))],
+        scratch_shapes=spread_sems(n, sum(len(pieces(x.shape[1])) for x in arrays))
+        + [pltpu.SemaphoreType.DMA((count,))],
         compiler_params=pltpu.CompilerParams(collective_id=0, has_side_effects=True),
         name="gather_queries",
     )(*arrays)
@@ -144,41 +155,31 @@
     )(rank, move_dst, keys, values)
 
 
-def unpack_kernel(blocks, n, cnt_ref, recv_ref, nk_in, nv_in, nk_ref, nv_ref, stage, at, sem, out_sem):
+def unpack_kernel(blocks, n, cnt_ref, recv_ref, nk_in, nv_in, nk_ref, nv_ref, blank, at, sem):
     at[0] = 0
+    blank[...] = jnp.zeros_like(blank)
     for src in range(n):
         for j in range(CAP):
 
             @pl.when((j < cnt_ref[src]) & (at[0] < n))
             def _():
-                for a in range(2):
-                    pltpu.make_async_copy(
-                        recv_ref.at[src * CAP + j, a], stage.at[a, at[0]], sem
-                    ).start()
+                for a, ref in enumerate((nk_ref, nv_ref)):
+                    pltpu.make_async_copy(recv_ref.at[src * CAP + j, a], ref.at[blocks + at[0]], sem).start()
                 at[0] = at[0] + 1
 
-    total = at[0]
-
-    def blank(k, _):
-        stage[:, k] = jnp.zeros_like(stage[:, k])
+    def clear(k, _):
+        for ref in (nk_ref, nv_ref):
+            pltpu.make_async_copy(blank, ref.at[blocks + k], sem).start()
         return 0
 
-    lax.fori_loop(total, n, blank, 0)
+    lax.fori_loop(at[0], n, clear, 0)
 
     def finish(k, _):
-        for a in range(2):
-            pltpu.make_async_copy(recv_ref.at[0, a], stage.at[a, 0], sem).wait()
+        for ref in (nk_ref, nv_ref):
+            pltpu.make_async_copy(blank, ref.at[blocks + k], sem).wait()
         return 0
 
-    lax.fori_loop(0, total, finish, 0)
-    outs = [
-        pltpu.make_async_copy(stage.at[a], ref.at[pl.ds(blocks, n)], out_sem.at[a])
-        for a, ref in enumerate((nk_ref, nv_ref))
-    ]
-    for c in outs:
-        c.start()
-    for c in outs:
-        c.wait()
+    lax.fori_loop(0, n, finish, 0)
 
 
 def unpack(n, blocks, arriving, received, new_keys, new_values):
@@ -186,14 +187,13 @@
     return pl.pallas_call(
         functools.partial(unpack_kernel, blocks, n),
         out_shape=[jax.ShapeDtypeStruct(x.shape, x.dtype) for x in (new_keys, new_values)],
-        in_specs=[SMEM, ANY, ANY, ANY],
+        in_specs=[SMEM, VMEM, ANY, ANY],
         out_specs=[ANY, ANY],
         input_output_aliases={2: 0, 3: 1},
         scratch_shapes=[
-            pltpu.VMEM((2, n, rows, lanes), new_keys.dtype),
+            pltpu.VMEM((rows, lanes), new_keys.dtype),
             pltpu.SMEM((1,), jnp.int32),
             pltpu.SemaphoreType.DMA,
-            pltpu.SemaphoreType.DMA((2,)),
         ],
         name="place_moves",
     )(arriving, received, new_keys, new_values)
@@ -352,7 +352,7 @@
     )(rank, block_req, block_idx, move_dst, lengths, dreq, q_all, keys, values, dk, dv, bias)
 
 
-def merge_parts(parts, out, level_out, heads, hd):
+def merge_parts(parts, out, level_out, heads, hd, after={}):
     levels = [level for _, level in parts]
     best = functools.reduce(jnp.maximum, levels)
     weights = [jnp.exp2(x - best) for x in levels]
@@ -366,6 +366,8 @@
             term = weight[:, h : h + 1] * view[:, cols].astype(jnp.float32)
             total = term if total is None else total + term
         out[:, cols] = total.astype(jnp.bfloat16)
+        if cols.stop in after:
+            after[cols.stop]()
     if level_out is not None:
         level_out[...] = best + jnp.log2(mass)
 
@@ -417,6 +419,33 @@
     for d in range(1, half):
         for c in far(d):
             c.wait_recv()
+    cuts = pieces(heads * hd)
+
+    def direct(d, p):
+        to = lax.rem(row + d, half) * 2 + side
+        return remote(
+            attn_own.at[:, cuts[p]], attn.at[me, :, cuts[p]], ds.at[p, d], dr.at[p, d], "ctx", to
+        )
+
+    def landed(d, other, only=None):
+        origin = lax.rem(row + half - d, half) * 2 + (1 - side if other else side)
+        sem = (ps, pr) if other else (ds, dr)
+        for p in range(len(cuts)) if only is None else [only]:
+            there = attn.at[origin, :, cuts[p]]
+            remote(there, there, sem[0].at[p, d], sem[1].at[p, d], "ctx", partner).wait_recv()
+
+    def share(p):
+        cut = cuts[p]
+        for d in range(1, half):
+            c = direct(d, p)
+            c.start()
+            sends.append(c)
+        c = remote(
+            attn_own.at[:, cut], attn.at[me, :, cut], ps.at[p, 0], pr.at[p, 0], "ctx", partner
+        )
+        c.start()
+        sends.append(c)
+
     merge_parts(
         [(o_ref.at[me], lse_ref[me]), (near_o.at[0], near_l[0])]
         + [(far_o.at[d], far_l[d]) for d in range(1, half)],
@@ -424,33 +453,19 @@
         None,
         heads,
         hd,
+        {cut.stop: functools.partial(share, p) for p, cut in enumerate(cuts)},
     )
     mine = pltpu.make_async_copy(attn_own, attn.at[me], local)
     mine.start()
 
-    def direct(d):
-        to = lax.rem(row + d, half) * 2 + side
-        return remote(attn_own, attn.at[me], ds.at[d], dr.at[d], "ctx", to)
-
-    def landed(d, other):
-        origin = lax.rem(row + half - d, half) * 2 + (1 - side if other else side)
-        sem = (ps, pr) if other else (ds, dr)
-        remote(attn_own, attn.at[origin], sem[0].at[d], sem[1].at[d], "ctx", partner).wait_recv()
-
-    for d in range(1, half):
-        c = direct(d)
-        c.start()
-        sends.append(c)
-    c = remote(attn_own, attn.at[me], ps.at[0], pr.at[0], "ctx", partner)
-    c.start()
-    sends.append(c)
-
     def pass_on(d):
-        landed(d, False)
         origin = lax.rem(row + half - d, half) * 2 + side
-        c = remote(attn.at[origin], attn.at[origin], ps.at[d], pr.at[d], "ctx", partner)
-        c.start()
-        sends.append(c)
+        for p in range(len(cuts)):
+            landed(d, False, p)
+            there = attn.at[origin, :, cuts[p]]
+            c = remote(there, there, ps.at[p, d], pr.at[p, d], "ctx", partner)
+            c.start()
+            sends.append(c)
 
     w = w_ref[...]
 
@@ -529,7 +544,7 @@
         ]
         + [dma((half,))] * 8
         + [dma((nh,))] * 2
-        + [dma((half,))] * 4
+        + [dma((len(pieces(cols)), half))] * 4
         + [dma],
         compiler_params=pltpu.CompilerParams(collective_id=1, has_side_effects=True),
         name="combine",
@@ -567,7 +582,8 @@
     if aligned:
         own = local_tokens // drafts
         dreq = me * own + jnp.arange(own, dtype=jnp.int32)
-        valid = jnp.full((own,), True)
+        valid = None
+        offs = lax.dynamic_slice_in_dim(draft_offs, me * own, own)
         (q_all,) = gather_all(n, [queries])
         dk, dv = draft_keys, draft_values
     else:
@@ -575,15 +591,16 @@
         dreq = me + n * jnp.arange(own, dtype=jnp.int32)
         valid = dreq < requests
         dreq = jnp.where(valid, dreq, 0)
+        offs = jnp.take(draft_offs, dreq, axis=0)
         q_all, dk, dv = gather_all(n, [queries, draft_keys, draft_values])
         dk, dv = dk.reshape(tokens, -1), dv.reshape(tokens, -1)
     sent, q_all = lax.optimization_barrier((sent, q_all))
     received = lax.all_to_all(sent, "ctx", split_axis=0, concat_axis=0, tiled=True)
     q_all = q_all.reshape(tokens, heads * hd)
-    offs = jnp.take(draft_offs, dreq, axis=0)
     line = jnp.arange(drafts, dtype=jnp.int32)
     seen = (line[None, None, :] >= offs[:, :, None]) & (line[None, None, :] <= line[None, :, None])
-    seen = seen & valid[:, None, None]
+    if valid is not None:
+        seen = seen & valid[:, None, None]
     same = jnp.arange(heads)[:, None] // (heads // kv) == jnp.arange(kv)[None, :]
     bias = jnp.where(
         seen[:, None, :, None, :] & same[None, :, None, :, None], 0.0, -1.0

time: 123 us -> 124 us (level)
  Pallas kernels: 111 us -> 113 us
where the time goes in v3:
time: 124 us; the launch traced here: 123 us
  Pallas kernels  113 us (91%)
  starting transfers between devices  3.94 us (3%)
  local copies, waits for them, and re-layouts  3.12 us (3%)
  other arithmetic  1.98 us (2%)
    pallas_call x1, Pallas kernels, combine(): pl.pallas_call(functools.partial(combine_kernel, dims), out_shape=jax.Sha...  67 us
    pallas_call x1, Pallas kernels, gather_all(): pl.pallas_call(functools.partial(gather_kernel, n, count), out_shape=[jax...  22.7 us
    pallas_call x1, Pallas kernels, attend(): pl.pallas_call(functools.partial(attend_kernel, dims), out_shape=[grown,...  16.7 us
    pallas_call x1, Pallas kernels, pack(): pl.pallas_call(functools.partial(pack_kernel, blocks, n), out_shape=jax.S...  4.01 us
    all_to_all x1, starting transfers between devices, shards(): lax.all_to_all(sent, 'ctx', split_axis=0, concat_axis=0, tiled=True)  3.94 us
    pallas_call x1, Pallas kernels, unpack(): pl.pallas_call(functools.partial(unpack_kernel, blocks, n), out_shape=[ja...  2.69 us
  transfers between devices with their start and end apart: 1, of which 0 were waited for; matrix products, arithmetic and copies ran while one was open for 3% of the time, Pallas kernels for 68%

profile of v3, /device:TPU:1, one launch (start us, length us, event | category | flops | bytes accessed | tf_op | source)
XLA Modules:
  0.0 123.0 jit_solution(18354312655171133772)
XLA Ops:
  0.6 0.0 copy-start
  0.6 22.7 %gather_queries.1 = bf16[8,48,1280]{2,1,0:T(8,128)(2,1)} custom-call(bf16[48,1280]{1,0:T(8,128)(2,1)} %refs_0_.1), custom_call_target="tpu_custom_call" | custom-call | tf_op jit(solution)/shard_map/gather_queries/pallas_call | solution.py:104
  23.4 4.0 %pack_moves.1 = bf16[16,2,256,128]{3,2,1,0:T(8,128)(2,1)} custom-call(s32[1]{0:T(128)} %bitcast.rank_ref, s32[512]{0:T(512)} %dst_ref.3, bf16[64,256,128]{2,1,0:T(8,128)(2,1)} %bitcast.12, bf16[64,256,128]{2,1,0:T(8,128)(2,1)} %bitcast.14), custom_call_target="tpu_custom_call" | custom-call | tf_op jit(solution)/shard_map/pack_moves/pallas_call | solution.py:148
  27.4 0.0 copy-start.3
  27.4 3.9 %all-to-all-start = ((bf16[16,2,256,128]{3,2,1,0:T(8,128)(2,1)}), bf16[16,2,256,128]{3,2,1,0:T(8,128)(2,1)S(1)}, u32[]{:S(2)}, u32[]{:S(2)}) async-start(bf16[16,2,256,128]{3,2,1,0:T(8,128)(2,1)} %pack_moves.1), calls=%async_computation | async-start | bytes 4194304 | tf_op jit(solution)/shard_map/all_to_all | solution.py:598
  31.4 0.1 reshape.106
  31.4 0.7 reduce_sum.9.cnt_ref
  32.1 0.1 constant_dynamic-slice_fusion
  32.2 0.1 copy.20
  32.3 0.1 and.47
  32.4 0.1 and.48
  32.6 0.1 copy.21
  32.7 0.1 and.44
  32.8 0.3 and.45
  33.1 0.2 copy.22
  33.3 0.5 iota_add_fusion.dreq_ref
  33.8 0.7 and_select_fusion.bias_ref
  34.5 16.7 %attend.1 = (bf16[72,256,128]{2,1,0:T(8,128)(2,1)}, bf16[72,256,128]{2,1,0:T(8,128)(2,1)}, bf16[384,1280]{1,0:T(8,128)(2,1)}, f32[384,128]{1,0:T(8,128)}) custom-call(s32[1]{0:T(128)} %bitcast.rank_ref, s32[512]{0:T(512)} %req_ref.1, s32[512]{0:T(512)} %idx_ref.1, s32[512]{0:T(512)} %dst_ref.3, s32[24]{0:T(128)} %len_ref.1, s32[3]{0:T(128)} %iota_add_fusion.dreq_ref, ...), custom_call_target="tpu_custom_call" | custom-call | flops 1342177280 | bytes 16777216 | tf_op jit(solution)/shard_map/attend/pallas_call | solution.py:332
  51.2 67.0 %combine.1 = bf16[96,640]{1,0:T(8,128)(2,1)} custom-call(bf16[8,48,1280]{2,1,0:T(8,128)(2,1)} %bitcast.19, f32[8,48,128]{2,1,0:T(8,128)} %bitcast.20, bf16[1280,640]{1,0:T(8,128)(2,1)} %w_ref.1), custom_call_target="tpu_custom_call" | custom-call | tf_op jit(solution)/shard_map/combine/pallas_call | solution.py:532
  118.3 0.0 all-to-all-done.recv_ref
  118.3 0.0 copy-start.1
  118.3 1.3 %copy-done.1 = bf16[16,2,256,128]{3,2,1,0:T(8,128)(2,1)} copy-done((bf16[16,2,256,128]{3,2,1,0:T(8,128)(2,1)}, bf16[16,2,256,128]{3,2,1,0:T(8,128)(2,1)S(1)}, u32[]{:S(2)}) %copy-start.1) | copy-done | bytes 2097176
  119.6 2.7 %place_moves.1 = (bf16[72,256,128]{2,1,0:T(8,128)(2,1)}, bf16[72,256,128]{2,1,0:T(8,128)(2,1)}) custom-call(s32[8]{0:T(128)} %reduce_sum.9.cnt_ref, bf16[16,2,256,128]{3,2,1,0:T(8,128)(2,1)} %copy-done.1, bf16[72,256,128]{2,1,0:T(8,128)(2,1)} %get-tuple-element.15.nk_in, ...), custom_call_target="tpu_custom_call", output_to_operand_aliasing={{0}: (2, {}), {1}: (3, {})} | custom-call | tf_op jit(solution)/shard_map/place_moves/pallas_call | solution.py:187
  122.3 0.7 copy.26
  (9 shorter events, 0.0 us)
Async XLA Ops:
  0.6 31.5 %copy-start = (s32[24,16]{0,1:T(8,128)S(1)}, s32[24,16]{0,1:T(8,128)}, u32[]{:S(2)}) copy-start(s32[24,16]{0,1:T(8,128)} %param.21) | copy-start | bytes 4612
  27.4 4.0 %copy-start.3 = (s32[512]{0:T(512)S(1)}, s32[512]{0:T(512)}, u32[]{:S(2)}) copy-start(s32[512]{0:T(512)} %dst_ref.3) | copy-start | bytes 6148
  27.4 90.9 %all-to-all-start = ((bf16[16,2,256,128]{3,2,1,0:T(8,128)(2,1)}), bf16[16,2,256,128]{3,2,1,0:T(8,128)(2,1)S(1)}, u32[]{:S(2)}, u32[]{:S(2)}) async-start(bf16[16,2,256,128]{3,2,1,0:T(8,128)(2,1)} %pack_moves.1), calls=%async_computation | async-start | bytes 4194304 | tf_op jit(solution)/shard_map/all_to_all | solution.py:598
  118.3 1.3 %copy-start.1 = (bf16[16,2,256,128]{3,2,1,0:T(8,128)(2,1)}, bf16[16,2,256,128]{3,2,1,0:T(8,128)(2,1)S(1)}, u32[]{:S(2)}) copy-start(bf16[16,2,256,128]{3,2,1,0:T(8,128)(2,1)S(1)} %all-to-all-done.recv_ref) | copy-start | bytes 6291460
  119.6 2.7 %copy-start.2 = (bf16[96,640]{1,0:T(8,128)(2,1)S(1)}, bf16[96,640]{1,0:T(8,128)(2,1)}, u32[]{:S(2)}) copy-start(bf16[96,640]{1,0:T(8,128)(2,1)} %combine.1) | copy-start | bytes 368644
